TPU v7x, 256 devices: a whole 4x4x8 slice. The times are simulated.
256 devices in a mesh: pole: 4 (over y), row: 8 (over z_lo, x), col: 8 (over z_hi, core).
Axes of the slice: x: 4, y: 4, z: 8 (z_hi: 4, z_lo: 2; z = z_hi * 2 + z_lo), core: 2. Of those that a mesh axis runs over, the one named last changes fastest.
Arguments:
- found_inverse: bfloat16 [4, 2, 8192, 8, 8, 128], P('pole', None, 'row', None, 'col'), may hold values from -0.125 to 0.125
- l_panel: bfloat16 [4, 2, 8192, 512], P('pole', None, ('row', 'col')), may hold values from -1.5 to 1.5
- block_pattern: int32 [64, 4], P(('row', 'col')), may hold values 0 or 1
- sup_widths: int32 [4], replicated, may hold values from 1 to 128, 320 in all
- diag_inverse: bfloat16 [4, 2, 512, 128], P('pole'), may hold values from -6 to 6
- pole_weights: float32 [4, 2], P('pole'), may hold values from -4 to 4
Outputs:
- density: float32 [512, 8192], P('col', 'row')
- diagonal: float32 [512, 128], replicated
Inputs may be any that keep to these rules, and one draw needn't show every extreme that they name: `sup_widths`: one supernode has exactly 128 columns.
All inputs are finite; a program needn't handle non-finite values. No bound on the sum of `block_pattern` on one device may be relied on, other than what follows from the above.
Results may differ from a plain program's by a relative error of at most 0.0003.
Values may be sent and summed in bfloat16 or wider, within the bound.
A program may use at most 128 MiB of HBM per device.

v0:
```python
import jax
import jax.numpy as jnp
from jax import lax
from jax.sharding import PartitionSpec as P


def contract(left, right):
    return jnp.einsum("jk,ij->ki", left, right, preferred_element_type=jnp.float32)


def pair_product(left, right):
    return jnp.einsum("ika,kbi->kab", left, right, precision=lax.Precision.HIGHEST)


def per_device(found_inverse, l_panel, block_pattern, sup_widths, diag_inverse, pole_weights):
    slot_width = diag_inverse.shape[-1]
    total_cols = l_panel.shape[-1]
    supernodes = total_cols // slot_width
    row_count = lax.axis_size("row")
    col_count = lax.axis_size("col")
    row_index = lax.axis_index("row")
    col_index = lax.axis_index("col")
    columns = jnp.arange(total_cols, dtype=jnp.int32)
    column_ok = columns % slot_width < jnp.repeat(sup_widths, slot_width)
    block_ok = jnp.repeat(block_pattern[0], slot_width) == 1
    masked = jnp.where(
        (column_ok & block_ok)[None, None, :], l_panel[0], jnp.zeros((), jnp.bfloat16)
    )
    everything = lax.all_gather(masked, ("row", "col"), axis=1, tiled=True)
    own_rows = lax.dynamic_slice_in_dim(
        everything, row_index * col_count * slot_width, col_count * slot_width, 1
    )
    grouped = everything.reshape(2, row_count, col_count, slot_width, total_cols)
    picked = lax.dynamic_index_in_dim(grouped, col_index, 2, keepdims=False)
    column_rows = picked.reshape(2, row_count * slot_width, total_cols)
    local_rows = found_inverse.shape[2]
    inverse = found_inverse[0].reshape(2, local_rows, row_count * slot_width)
    part_real = contract(column_rows[1], inverse[1]) - contract(column_rows[0], inverse[0])
    part_imag = -(contract(column_rows[1], inverse[0]) + contract(column_rows[0], inverse[1]))
    w_real = pole_weights[0, 0]
    w_imag = pole_weights[0, 1]
    weighted = w_real * part_real - w_imag * part_imag
    whole = lax.psum(weighted, "pole")
    density = lax.psum_scatter(whole, "col", scatter_dimension=0, tiled=True)
    lifted = own_rows.astype(jnp.float32).reshape(2, local_rows, supernodes, slot_width)
    upper_real = part_real.reshape(supernodes, slot_width, local_rows)
    upper_imag = part_imag.reshape(supernodes, slot_width, local_rows)
    t_real = pair_product(lifted[0], upper_real) - pair_product(lifted[1], upper_imag)
    t_imag = pair_product(lifted[0], upper_imag) + pair_product(lifted[1], upper_real)
    lead_flag = ((row_index == 0) & (col_index == 0)).astype(jnp.float32)
    d_real = diag_inverse[0, 0].astype(jnp.float32).reshape(supernodes, slot_width, slot_width)
    d_imag = diag_inverse[0, 1].astype(jnp.float32).reshape(supernodes, slot_width, slot_width)
    local_term = lead_flag * (w_real * d_real - w_imag * d_imag) - (
        w_real * t_real - w_imag * t_imag
    )
    diagonal = lax.psum(local_term.reshape(total_cols, slot_width), ("pole", "row", "col"))
    return (density, diagonal)


def solution(mesh):
    in_specs = (
        P("pole", None, "row", None, "col", None),
        P("pole", None, ("row", "col"), None),
        P(("row", "col"), None),
        P(),
        P("pole", None, None, None),
        P("pole", None),
    )
    out_specs = (P("col", "row"), P())
    return jax.shard_map(
        per_device, mesh=mesh, in_specs=in_specs, out_specs=out_specs, check_vma=False
    )
```

profile of v0, /device:TPU:2, one launch (start us, length us, event | category | flops | bytes accessed | tf_op | source)
XLA Modules:
  0.0 514.2 jit_solution(14721515015720495059)
XLA Ops:
  7.2 0.0 all-gather.2.cloned.1.call-start
  7.2 0.7 compare_bitcast_fusion
  7.9 0.7 fusion.25
  8.6 1.7 bitcast_select_fusion
  10.3 0.0 all-gather.2.cloned.1.call-update
  10.3 0.0 reduce-scatter.2.cloned.1.call-start
  10.4 1.3 fusion.27
  11.7 3.8 fusion.26
  15.5 127.3 %all-gather.2.cloned.1.call-done = bf16[2,8192,512]{2,1,0:T(8,128)(2,1)} async-done(((bf16[2,128,512]{2,1,0:T(8,128)(2,1)}), bf16[2,8192,512]{2,1,0:T(8,128)(2,1)}) %all-gather.2.cloned.1.call-update) | async-done | bytes 16777232 | tf_op jit(solution)/shard_map/all_gather | solution.py:29
  142.8 1.7 constant_dynamic-slice_fusion.3
  144.6 1.3 fusion
  145.9 0.0 copy-start.2
  145.9 1.3 fusion.2
  147.2 0.3 copy-done.2
  147.5 1.3 fusion.12
  148.8 4.6 multiply_subtract_fusion
  153.4 0.0 copy-start.3
  153.4 0.0 reduce-scatter.2.cloned.1.call-update
  153.4 0.0 all-reduce.3.cloned.1.call-start
  153.4 0.9 copy-done.3
  154.3 1.3 subtract_multiply_fusion
  155.6 3.0 constant_dynamic-slice_fusion.2
  158.6 1.5 copy.9
  160.1 2.3 copy.8
  162.3 0.0 copy-start.1
  162.3 3.3 fusion.29
  165.7 0.0 copy-start
  165.7 0.0 copy-done.1
  165.7 1.2 fusion.28
  166.9 0.4 copy-done
  167.3 1.9 fusion.20
  169.1 2.5 fusion.19
  171.6 0.0 all-reduce.3.cloned.1.call-update
  171.6 0.0 all-reduce.5.cloned.1.call-start
  171.7 25.0 %reduce-scatter.2.cloned.1.call-done = f32[64,1024]{1,0:T(8,128)} async-done(((f32[512,1024]{1,0:T(8,128)}), f32[64,1024]{1,0:T(8,128)}) %reduce-scatter.2.cloned.1.call-update) | async-done | bytes 262160 | tf_op jit(solution)/shard_map/reduce_scatter | solution.py:44
  196.7 0.0 all-reduce.5.cloned.1.call-update
  196.7 259.6 %all-reduce.3.cloned.1.call-done = f32[512,128]{1,0:T(8,128)} async-done(((f32[512,128]{1,0:T(8,128)}), f32[512,128]{1,0:T(8,128)}) %all-reduce.3.cloned.1.call-update) | async-done | bytes 262160 | tf_op jit(solution)/shard_map/psum | solution.py:56
  456.3 48.0 %all-reduce.5.cloned.1.call-done = f32[64,1024]{1,0:T(8,128)} async-done(((f32[64,1024]{1,0:T(8,128)}), f32[64,1024]{1,0:T(8,128)}) %all-reduce.5.cloned.1.call-update) | async-done | bytes 262160 | tf_op jit(solution)/shard_map/psum | solution.py:43
  504.3 1.7 copy.36
  506.0 1.7 copy.37
Async XLA Ops:
  7.2 135.7 %all-gather.2.cloned.1.call-start = ((), (), s32[]{:S(2)}) async-start(), calls=%async_computation.1 | async-start | bytes 17039360 | tf_op jit(solution)/shard_map/all_gather | solution.py:29
  10.3 186.4 %reduce-scatter.2.cloned.1.call-start = ((), (), s32[]{:S(2)}) async-start(), calls=%async_computation.3 | async-start | bytes 2359296 | tf_op jit(solution)/shard_map/reduce_scatter | solution.py:44
  145.9 1.6 copy-start.2
  153.4 0.9 copy-start.3
  153.4 302.9 %all-reduce.3.cloned.1.call-start = ((), (), s32[]{:S(2)}) async-start(), calls=%async_computation.2 | async-start | bytes 524288 | tf_op jit(solution)/shard_map/psum | solution.py:56
  162.3 3.3 copy-start.1
  165.7 1.6 copy-start
  171.6 332.7 %all-reduce.5.cloned.1.call-start = ((), (), s32[]{:S(2)}) async-start(), calls=%async_computation.4 | async-start | bytes 524288 | tf_op jit(solution)/shard_map/psum | solution.py:43
Sparse Core Ops, SparseCore 0:
  10.4 132.3 all-gather.1
  153.5 43.1 reduce-scatter.1
  202.7 253.5 all-reduce.2
  458.5 45.7 all-reduce.4
where the time goes:
time: 515 us; the launch traced here: 514 us
  waiting for transfers between devices  460 us (89%)
  local copies, waits for them, and re-layouts  18.5 us (4%)
  matrix products  17.3 us (3%)
  between operations  13.9 us (3%)
    psum x1, waiting for transfers between devices, per_device(): lax.psum(local_term.reshape(total_cols, slot_width), ('pole', 'row', 'col'))  260 us
    all_gather x1, waiting for transfers between devices, per_device(): everything = lax.all_gather(masked, ('row', 'col'), axis=1, tiled=True)  127 us
    psum x1, waiting for transfers between devices, per_device(): whole = lax.psum(weighted, 'pole')  48 us
    reduce_scatter x1, waiting for transfers between devices, per_device(): density = lax.psum_scatter(whole, 'col', scatter_dimension=0, tiled=True)  25 us
  transfers between devices with their start and end apart: 4, of which 4 were waited for; matrix products, arithmetic and copies ran while one was open for 4% of the time, Pallas kernels for 0%

commit v1 on v0

--- a/solution.py
+++ b/solution.py
@@ -53,7 +53,9 @@
     local_term = lead_flag * (w_real * d_real - w_imag * d_imag) - (
         w_real * t_real - w_imag * t_imag
     )
-    diagonal = lax.psum(local_term.reshape(total_cols, slot_width), ("pole", "row", "col"))
+    diagonal = local_term.reshape(total_cols, slot_width)
+    for src_i in (("row", "col"), "pole"):
+        diagonal = jax.lax.psum(diagonal, src_i)
     return (density, diagonal)
 
 

time: 515 us -> 444 us (0.86)
  waiting for transfers between devices: 460 us -> 395 us
    psum x1, waiting for transfers between devices: 260 us -> 174 us  [per_device(): diagonal = jax.lax.psum(diagonal, src_i)]
    reduce_scatter x1, waiting for transfers between devices: 25 us -> 45.1 us  [per_device(): density = lax.psum_scatter(whole, 'col', scatter_dimension=0, tiled=True)]
  transfers between devices with their start and end apart: 4 -> 4, of which waited for: 4 -> 4; matrix products, arithmetic and copies ran while one was open for 4% -> 2% of each run, Pallas kernels for 0% -> 0%
where the time goes in v1:
time: 444 us
  waiting for transfers between devices  395 us (89%)
  matrix products  14.7 us (3%)
  local copies, waits for them, and re-layouts  14.4 us (3%)
  between operations  13.9 us (3%)
  other arithmetic  5.4 us (1%)
    psum x1, waiting for transfers between devices, per_device(): diagonal = jax.lax.psum(diagonal, src_i)  174 us
    all_gather x1, waiting for transfers between devices, per_device(): everything = lax.all_gather(masked, ('row', 'col'), axis=1, tiled=True)  124 us
    psum x1, waiting for transfers between devices, per_device(): whole = lax.psum(weighted, 'pole')  50.6 us
    reduce_scatter x1, waiting for transfers between devices, per_device(): density = lax.psum_scatter(whole, 'col', scatter_dimension=0, tiled=True)  45.1 us
  transfers between devices with their start and end apart: 4, of which 4 were waited for; matrix products, arithmetic and copies ran while one was open for 2% of the time, Pallas kernels for 0%

profile of v1, /device:TPU:2, one launch (start us, length us, event | category | flops | bytes accessed | tf_op | source)
XLA Modules:
  0.0 443.8 jit_solution(14336903163932519314)
XLA Ops:
  7.2 0.0 all-gather.2.cloned.1.call-start
  7.2 0.7 compare_bitcast_fusion
  7.9 0.7 fusion.25
  8.6 1.7 bitcast_select_fusion
  10.3 0.0 all-gather.2.cloned.1.call-update
  10.3 0.0 all-reduce.4.cloned.1.call-start
  10.4 1.4 fusion.27
  11.7 2.3 subtract_multiply_fusion
  14.1 4.4 %fusion.26 = (bf16[1,1,1024,8,1,128]{5,3,4,2,1,0:T(8,128)(2,1)}, bf16[1,1,1024,8,1,128]{5,3,4,2,1,0:T(8,128)(2,1)}) fusion(bf16[1,2,1024,8,1,128]{5,3,4,2,1,0:T(8,128)(2,1)} %param.6), kind=kLoop, calls=%fused_computation.35 | loop fusion | bytes 8388608 | tf_op jit(solution)/shard_map/slice | solution.py:38
  18.5 124.3 %all-gather.2.cloned.1.call-done = bf16[2,8192,512]{2,1,0:T(8,128)(2,1)} async-done(((bf16[2,128,512]{2,1,0:T(8,128)(2,1)}), bf16[2,8192,512]{2,1,0:T(8,128)(2,1)}) %all-gather.2.cloned.1.call-update) | async-done | bytes 16777232 | tf_op jit(solution)/shard_map/all_gather | solution.py:29
  142.8 1.7 constant_dynamic-slice_fusion.2
  144.5 0.5 copy.9
  145.0 0.5 copy.8
  145.6 0.0 copy-start.1
  145.6 1.9 constant_dynamic-slice_fusion.3
  147.5 0.3 copy-done.1
  147.8 1.3 fusion
  149.1 0.0 copy-start
  149.1 1.3 fusion.2
  150.4 0.3 copy-done
  150.7 1.3 fusion.12
  152.0 4.1 multiply_subtract_fusion
  156.1 1.2 fusion.29
  157.3 1.2 fusion.28
  158.4 1.8 fusion.20
  160.3 2.6 fusion.19
  162.9 0.0 all-reduce.4.cloned.1.call-update
  162.9 0.0 reduce-scatter.2.cloned.1.call-start
  162.9 0.7 reduce-scatter.2.cloned.1.call-update
  163.6 0.0 all-reduce.6.cloned.1.call-start
  163.7 174.5 %all-reduce.4.cloned.1.call-done = f32[512,128]{1,0:T(8,128)} async-done(((f32[512,128]{1,0:T(8,128)}), f32[512,128]{1,0:T(8,128)}) %all-reduce.4.cloned.1.call-update) | async-done | bytes 262160 | tf_op jit(solution)/shard_map/psum | solution.py:58
  338.2 45.1 %reduce-scatter.2.cloned.1.call-done = f32[64,1024]{1,0:T(8,128)} async-done(((f32[512,1024]{1,0:T(8,128)}), f32[64,1024]{1,0:T(8,128)}) %reduce-scatter.2.cloned.1.call-update) | async-done | bytes 262160 | tf_op jit(solution)/shard_map/reduce_scatter | solution.py:44
  383.3 0.0 all-reduce.6.cloned.1.call-update
  383.3 50.6 %all-reduce.6.cloned.1.call-done = (f32[64,1024]{1,0:T(8,128)}, f32[512,128]{1,0:T(8,128)}) async-done(((f32[64,1024]{1,0:T(8,128)}, f32[512,128]{1,0:T(8,128)}), (f32[64,1024]{1,0:T(8,128)}, f32[512,128]{1,0:T(8,128)})) %all-reduce.6.cloned.1.call-update) | async-done | bytes 524304 | tf_op jit(solution)/shard_map/psum | solution.py:43
  433.9 1.7 copy.37
  435.6 1.7 copy.38
Async XLA Ops:
  7.2 135.7 %all-gather.2.cloned.1.call-start = ((), (), s32[]{:S(2)}) async-start(), calls=%async_computation.1 | async-start | bytes 17039360 | tf_op jit(solution)/shard_map/all_gather | solution.py:29
  10.3 327.9 %all-reduce.4.cloned.1.call-start = ((), (), s32[]{:S(2)}) async-start(), calls=%async_computation.2 | async-start | bytes 524288 | tf_op jit(solution)/shard_map/psum | solution.py:58
  145.6 2.2 copy-start.1
  149.1 1.6 copy-start
  162.9 220.4 %reduce-scatter.2.cloned.1.call-start = ((), (), s32[]{:S(2)}) async-start(), calls=%async_computation.3 | async-start | bytes 2359296 | tf_op jit(solution)/shard_map/reduce_scatter | solution.py:44
  163.6 270.3 %all-reduce.6.cloned.1.call-start = ((), (), s32[]{:S(2)}) async-start(), calls=%async_computation.4 | async-start | bytes 1048576 | tf_op jit(solution)/shard_map/psum | solution.py:43
Sparse Core Ops, SparseCore 0:
  10.4 132.3 all-gather.1
  163.0 175.1 all-reduce.3
  340.7 42.5 reduce-scatter.1
  385.6 48.2 all-reduce.5
